TPU v7x, 32 devices: a whole 2x2x4 slice. The times are simulated.
32 devices in a mesh: req: 16 (over z, x, core), tp: 2 (over y).
Axes of the slice: x: 2, y: 2, z: 4, core: 2. Of those that a mesh axis runs over, the one named last changes fastest.
Arguments:
- x_in: bfloat16 [2048, 8192], P('req', 'tp'), may hold values from -6 to 6
- z_gate: bfloat16 [2048, 8192], P('req', 'tp'), may hold values from -6 to 6
- conv_edge: bfloat16 [128, 3, 8192], P('req', None, 'tp'), may hold values from -6 to 6
- conv_weight: float32 [4, 8192], P(None, 'tp'), may hold values from -3 to 3
- conv_bias: float32 [8192], P('tp'), may hold values from -3 to 3
- x_proj_weight: bfloat16 [8192, 288], P('tp'), may hold values from -0.0625 to 0.0625
- dt_gain: float32 [256], replicated, may hold values from 0.5 to 1.5
- b_gain: float32 [16], replicated, may hold values from 0.5 to 1.5
- c_gain: float32 [16], replicated, may hold values from 0.5 to 1.5
- dt_proj_weight: bfloat16 [256, 8192], P(None, 'tp'), may hold values from -0.375 to 0.375
- dt_bias: float32 [8192], P('tp'), may hold values from -6 to -2
- a_log: float32 [16, 8192], P(None, 'tp'), may hold values from 0 to 3
- skip: float32 [8192], P('tp'), may hold values from 0.5 to 1.5
- ssm_state: bfloat16 [128, 16, 8192], P('req', None, 'tp'), may hold values from -6 to 6
- accepted: int32 [128], P('req'), may hold values from 0 to 16, as said below
- prompt_len: int32 [128], P('req'), may hold values from 1 to 8192, 131072 in all
- tenant_range: int32 [4, 2], replicated, may hold values from 0 to 128, as said below
- owner: int32 [128], replicated, may hold values from 0 to 15, as said below
Outputs:
- mixed_out: bfloat16 [2048, 8192], P('req', 'tp')
- owned_state: bfloat16 [192, 16, 8192], P('req', None, 'tp')
- owned_edge: bfloat16 [192, 3, 8192], P('req', None, 'tp')
- tenant_stats: float32 [4, 2], replicated
Inputs may be any that keep to these rules, and one draw needn't show every extreme that they name: `accepted`: accepted draft tokens; the largest value 16 occurs in every draw. `tenant_range`: the rows cover all requests in order, row k starting where row k - 1 ends; every tenant has at least one request. The 8 requests of one device go to 8 different owners; at most 12 requests go to one owner, and some owner receives exactly 12 in every draw.
All inputs are finite; a program needn't handle non-finite values. No bound on the sum of `prompt_len` on one device may be relied on, other than what follows from the above.
Results may differ from a plain program's by a relative error of at most 0.0085.
Values may be sent and summed in bfloat16 or wider, within the bound.
No kernel may reach another device: no remote copies, remote signals or barrier semaphores. Data moves between devices by JAX's collectives and lax.ppermute only.
A program may use at most 64 MiB of HBM per device.

v0:
```python
import jax
import jax.numpy as jnp
from jax import lax
from jax.sharding import PartitionSpec as P

STEPS = 16
PAIR_MOST = 1
EPSILON = 1e-06
SQUARE_FLOOR = 0.25


def rms_scaled(values, scale_gain, floor_value, eps_value):
    square = jnp.mean(values * values, axis=-1, keepdims=True)
    return values * lax.rsqrt(jnp.maximum(square, floor_value) + eps_value) * scale_gain


def normalize(projected, dt_gain, b_gain, c_gain):
    rank_cols = dt_gain.shape[0]
    state_cols = b_gain.shape[0]
    dt_low = rms_scaled(projected[:, :rank_cols], dt_gain, 0.0, EPSILON).astype(jnp.bfloat16)
    input_map = rms_scaled(
        projected[:, rank_cols : rank_cols + state_cols], b_gain, SQUARE_FLOOR, 0.0
    ).astype(jnp.bfloat16)
    output_map = rms_scaled(
        projected[:, rank_cols + state_cols :], c_gain, SQUARE_FLOOR, 0.0
    ).astype(jnp.bfloat16)
    return (dt_low, input_map, output_map)


def per_device(
    x_in,
    z_gate,
    conv_edge,
    conv_weight,
    conv_bias,
    x_proj_weight,
    dt_gain,
    b_gain,
    c_gain,
    dt_proj_weight,
    dt_bias,
    a_log,
    skip,
    ssm_state,
    accepted,
    prompt_len,
    tenant_range,
    owner,
):
    per_dev = ssm_state.shape[0]
    channels = x_in.shape[1]
    drafts = x_in.shape[0] // per_dev
    taps = conv_weight.shape[0]
    state_size = ssm_state.shape[1]
    owners = lax.axis_size("req")
    device = lax.axis_index("req")
    own_most = min(per_dev + per_dev // 2, owners)
    window = jnp.concatenate([conv_edge, x_in.reshape(per_dev, drafts, channels)], axis=1)
    lag_index = accepted[:, None] + jnp.arange(taps - 1, dtype=jnp.int32)[None, :]
    kept_edge = jnp.take_along_axis(window, lag_index[:, :, None], axis=1)
    my_owners = lax.dynamic_slice_in_dim(owner, device * per_dev, per_dev)
    local_ids = jnp.arange(per_dev, dtype=jnp.int32)
    earlier = jnp.sum(
        (my_owners[None, :] == my_owners[:, None]) & (local_ids[None, :] < local_ids[:, None]),
        axis=1,
    )
    send_slot = my_owners * PAIR_MOST + earlier

    def place_rows(payload):
        blank_rows = jnp.zeros((owners * PAIR_MOST,) + payload.shape[1:], payload.dtype)
        return blank_rows.at[send_slot].set(payload)

    route_table = owner.reshape(owners, per_dev)
    incoming = jnp.sum((route_table == device).astype(jnp.int32), axis=1)
    occupied = (jnp.arange(PAIR_MOST, dtype=jnp.int32)[None, :] < incoming[:, None]).reshape(-1)
    target = jnp.where(occupied, jnp.cumsum(occupied.astype(jnp.int32)) - 1, own_most)

    def settle_rows(payload):
        blank_rows = jnp.zeros((own_most,) + payload.shape[1:], payload.dtype)
        return blank_rows.at[target].set(payload, mode="drop")

    summed = jnp.zeros((per_dev, drafts, channels), jnp.float32) + conv_bias
    for offset in range(taps):
        summed = summed + conv_weight[offset] * window[:, offset : offset + drafts, :].astype(
            jnp.float32
        )
    conv_out = jax.nn.silu(summed).astype(jnp.bfloat16)
    flattened = conv_out.reshape(per_dev * drafts, channels)
    partial_proj = jnp.dot(flattened, x_proj_weight, preferred_element_type=jnp.float32)
    projected = lax.psum(partial_proj, "tp")
    dt_low, input_map, output_map = normalize(projected, dt_gain, b_gain, c_gain)
    step_size = jax.nn.softplus(
        jnp.dot(dt_low, dt_proj_weight, preferred_element_type=jnp.float32) + dt_bias
    )
    step_size = step_size.reshape(per_dev, drafts, channels)
    decay_rate = -jnp.exp(a_log)
    conv_float = conv_out.astype(jnp.float32)
    in_float = input_map.astype(jnp.float32).reshape(per_dev, drafts, state_size)
    out_float = output_map.astype(jnp.float32).reshape(per_dev, drafts, state_size)
    initial = ssm_state.astype(jnp.float32)
    kept_first = jnp.where((accepted == 0)[:, None, None], initial, jnp.zeros_like(initial))

    def advance(running, position):
        hidden, kept_state = running
        size_now = step_size[:, position, :]
        conv_now = conv_float[:, position, :]
        decay_now = jnp.exp(size_now[:, None, :] * decay_rate[None, :, :])
        hidden = (
            decay_now * hidden + (size_now * conv_now)[:, None, :] * in_float[:, position, :, None]
        )
        output_now = jnp.sum(out_float[:, position, :, None] * hidden, axis=1) + skip * conv_now
        kept_state = jnp.where((accepted == position + 1)[:, None, None], hidden, kept_state)
        return ((hidden, kept_state), output_now)

    (last_state, kept_state), per_step = lax.scan(
        advance, (initial, kept_first), jnp.arange(drafts, dtype=jnp.int32)
    )
    kept_state = kept_state.astype(jnp.bfloat16)
    received_state, received_edge = (
        lax.all_to_all(place_rows(kept_state), "req", split_axis=0, concat_axis=0, tiled=True),
        lax.all_to_all(place_rows(kept_edge), "req", split_axis=0, concat_axis=0, tiled=True),
    )
    scan_out = jnp.transpose(per_step, (1, 0, 2))
    gate_float = z_gate.reshape(per_dev, drafts, channels).astype(jnp.float32)
    mixed_out = (
        (scan_out * jax.nn.silu(gate_float))
        .astype(jnp.bfloat16)
        .reshape(per_dev * drafts, channels)
    )
    owned_state = settle_rows(received_state)
    owned_edge = settle_rows(received_edge)
    global_ids = device * per_dev + local_ids
    inside = (global_ids[None, :] >= tenant_range[:, 0:1]) & (
        global_ids[None, :] < tenant_range[:, 1:2]
    )
    accepted_float = accepted.astype(jnp.float32)
    new_length = (prompt_len + accepted + 1).astype(jnp.float32)
    accept_sum = jnp.sum(jnp.where(inside, accepted_float[None, :], 0.0), axis=1)
    length_sum = jnp.sum(jnp.where(inside, new_length[None, :], 0.0), axis=1)
    partial_sums = jnp.stack([accept_sum, length_sum], axis=1)
    totals = lax.psum(partial_sums, "req")
    members = (tenant_range[:, 1] - tenant_range[:, 0]).astype(jnp.float32)
    accept_rate = totals[:, 0] / (STEPS * members)
    length_load = totals[:, 1] / members / (jnp.sum(totals[:, 1]) / jnp.sum(members))
    tenant_stats = jnp.stack([accept_rate, length_load], axis=1)
    return (mixed_out, owned_state, owned_edge, tenant_stats)


def solution(mesh):
    placed = (
        P("req", "tp"),
        P("req", "tp"),
        P("req", None, "tp"),
        P(None, "tp"),
        P("tp"),
        P("tp", None),
        P(),
        P(),
        P(),
        P(None, "tp"),
        P("tp"),
        P(None, "tp"),
        P("tp"),
        P("req", None, "tp"),
        P("req"),
        P("req"),
        P(),
        P(),
    )
    return jax.shard_map(
        per_device,
        mesh=mesh,
        in_specs=placed,
        out_specs=(P("req", "tp"), P("req", None, "tp"), P("req", None, "tp"), P()),
        check_vma=False,
    )
```

profile of v0, /device:TPU:16, one launch (start us, length us, event | category | flops | bytes accessed | tf_op | source)
XLA Modules:
  0.0 362.7 jit_solution(11368662169548580320)
XLA Ops:
  22.2 6.1 %all-to-all-start.1 = ((bf16[16,3,4096]{2,1,0:T(4,128)(2,1)}), bf16[16,3,4096]{2,1,0:T(4,128)(2,1)}, u32[]{:S(2)}, u32[]{:S(2)}) async-start(bf16[16,3,4096]{2,1,0:T(4,128)(2,1)} %scatter_fusion.2), calls=%async_computation.1 | async-start | bytes 1048576 | tf_op jit(solution)/shard_map/all_to_all | solution.py:121
  32.0 6.9 %all-reduce.2.cloned.1.call-done = f32[128,288]{0,1:T(8,128)} async-done(((f32[128,288]{0,1:T(8,128)}), f32[128,288]{0,1:T(8,128)}) %all-reduce.2.cloned.1.call-update) | async-done | bytes 147472 | tf_op jit(solution)/shard_map/psum | solution.py:90
  42.4 4.5 %compare_select_fusion = f32[128,4096]{1,0:T(8,128)} fusion(bf16[256,4096]{1,0:T(8,128)(2,1)} %param.29, f32[4096]{0:T(1024)} %param.30, f32[128,288]{0,1:T(8,128)} %all-reduce.2.cloned.1.call-done, f32[256]{0:T(256)} %param.26, f32[128]{0:T(128)S(1)} %add_rsqrt_fusion), kind=kOutput, calls=%fused_computation.17 | convolution fusion | flops 272203776 | bytes 4343296 | tf_op jit(solution)/shard_map/dot_general | solution.py:93
  47.0 212.8 %while.14 = (s32[]{:T(128)}, f32[8,16,4096]{2,1,0:T(8,128)}, bf16[8,16,4096]{2,1,0:T(8,128)(2,1)S(1)}, f32[16,8,4096]{2,1,0:T(8,128)}, s32[16]{0:T(128)S(1)}, /*...) while((s32[]{:T(128)}, f32[8,16,4096]{2,1,0:T(8,128)}, ...), condition=%wide.region_6.7_spmd, body=%wide.region_4.6_spmd.sunk | while | flops 3735566 | bytes 10243851 | solution.py:115
  52.5 3.5 multiply_reduce_fusion.5
  65.8 3.5 multiply_reduce_fusion.5
  79.1 3.5 multiply_reduce_fusion.5
  92.4 3.5 multiply_reduce_fusion.5
  105.7 3.5 multiply_reduce_fusion.5
  119.0 3.5 multiply_reduce_fusion.5
  132.3 3.5 multiply_reduce_fusion.5
  145.6 3.5 multiply_reduce_fusion.5
  158.9 3.5 multiply_reduce_fusion.5
  172.2 3.5 multiply_reduce_fusion.5
  185.5 3.5 multiply_reduce_fusion.5
  198.8 3.5 multiply_reduce_fusion.5
  212.1 3.5 multiply_reduce_fusion.5
  225.4 3.5 multiply_reduce_fusion.5
  238.7 3.5 multiply_reduce_fusion.5
  252.0 3.5 multiply_reduce_fusion.5
  264.2 6.2 %all-to-all-start = ((bf16[16,16,4096]{2,1,0:T(8,128)(2,1)}), bf16[16,16,4096]{2,1,0:T(8,128)(2,1)}, u32[]{:S(2)}, u32[]{:S(2)}) async-start(bf16[16,16,4096]{2,1,0:T(8,128)(2,1)} %scatter_fusion), calls=%async_computation | async-start | bytes 4194304 | tf_op jit(solution)/shard_map/all_to_all | solution.py:120
  270.7 65.5 %psum.15 = f32[4,2]{0,1:T(2,128)S(1)} all-reduce(f32[4,2]{0,1:T(2,128)S(1)} %pad_maximum_fusion), channel_id=1, replica_groups=mesh['req'=16,'tp'=2] {'req'}, use_global_device_ids=true, to_apply=%region_16.17 | all-reduce | flops 8 | bytes 64 | tf_op jit(solution)/shard_map/psum | solution.py:141
  341.4 3.6 fusion.2
  350.1 5.8 %scatter_fusion.1 = bf16[12,16,4096]{2,1,0:T(8,128)(2,1)} fusion(bf16[12,16,4096]{2,1,0:T(8,128)(2,1)} %broadcast_in_dim.97, s32[16]{0:T(128)S(1)} %fusion.5, bf16[16,16,4096]{2,1,0:T(8,128)(2,1)} %all-to-all-done), kind=kCustom, calls=%fused_computation.2 | custom fusion | bytes 6291520 | tf_op jit(solution)/shard_map/scatter | solution.py:80
  (201 shorter events, 150.2 us)
Async XLA Ops:
  7.2 7.3 %copy-start = (bf16[4096,288]{0,1:T(8,128)(2,1)S(1)}, bf16[4096,288]{0,1:T(8,128)(2,1)}, u32[]{:S(2)}) copy-start(bf16[4096,288]{0,1:T(8,128)(2,1)} %param.25) | copy-start | bytes 7077892
  7.2 4.0 %copy-start.2 = (bf16[128,4096]{1,0:T(8,128)(2,1)S(1)}, bf16[128,4096]{1,0:T(8,128)(2,1)}, u32[]{:S(2)}) copy-start(bf16[128,4096]{1,0:T(8,128)(2,1)} %param.20) | copy-start | bytes 3145732
  7.2 4.0 %copy-start.7 = (f32[4096]{0:T(1024)S(1)}, f32[4096]{0:T(1024)}, u32[]{:S(2)}) copy-start(f32[4096]{0:T(1024)} %param.24) | copy-start | bytes 49156
  7.2 31.7 %all-reduce.2.cloned.1.call-start = ((), (), s32[]{:S(2)}) async-start(), calls=%async_computation.2 | async-start | bytes 294912 | tf_op jit(solution)/shard_map/psum | solution.py:90
  11.2 2.7 copy-start.1
  14.4 1.5 copy-start.9
  14.5 1.7 copy-start.13
  22.2 242.1 %all-to-all-start.1 = ((bf16[16,3,4096]{2,1,0:T(4,128)(2,1)}), bf16[16,3,4096]{2,1,0:T(4,128)(2,1)}, u32[]{:S(2)}, u32[]{:S(2)}) async-start(bf16[16,3,4096]{2,1,0:T(4,128)(2,1)} %scatter_fusion.2), calls=%async_computation.1 | async-start | bytes 1048576 | tf_op jit(solution)/shard_map/all_to_all | solution.py:121
  28.3 2.9 copy-start.6
  28.3 11.4 %copy-start.10 = (f32[16]{0:T(128)S(1)}, f32[16]{0:T(128)}, u32[]{:S(2)}) copy-start(f32[16]{0:T(128)} %param.28) | copy-start | bytes 196
  28.3 11.3 %copy-start.11 = (f32[16]{0:T(128)S(1)}, f32[16]{0:T(128)}, u32[]{:S(2)}) copy-start(f32[16]{0:T(128)} %param.27) | copy-start | bytes 196
  42.4 4.6 %copy-start.5 = (f32[4096]{0:T(1024)S(1)}, f32[4096]{0:T(1024)}, u32[]{:S(2)}) copy-start(f32[4096]{0:T(1024)} %param.32) | copy-start | bytes 49156
  264.2 6.2 %copy-start.8 = (s32[4,2]{0,1:T(2,128)S(1)}, s32[4,2]{0,1:T(2,128)}, u32[]{:S(2)}) copy-start(s32[4,2]{0,1:T(2,128)} %param.36) | copy-start | bytes 100
  264.2 6.2 %copy-start.12 = (s32[8]{0:T(128)S(1)}, s32[8]{0:T(128)}, u32[]{:S(2)}) copy-start(s32[8]{0:T(128)} %param.35) | copy-start | bytes 100
  264.2 72.0 %copy-start.14 = (s32[128]{0:T(128)S(1)}, s32[128]{0:T(128)}, u32[]{:S(2)}) copy-start(s32[128]{0:T(128)} %param.37) | copy-start | bytes 1540
  264.2 72.4 %copy-start.4 = (bf16[128,4096]{1,0:T(8,128)(2,1)S(1)}, bf16[128,4096]{1,0:T(8,128)(2,1)}, u32[]{:S(2)}) copy-start(bf16[128,4096]{1,0:T(8,128)(2,1)} %param.21) | copy-start | bytes 3145732
  264.2 84.6 %all-to-all-start = ((bf16[16,16,4096]{2,1,0:T(8,128)(2,1)}), bf16[16,16,4096]{2,1,0:T(8,128)(2,1)}, u32[]{:S(2)}, u32[]{:S(2)}) async-start(bf16[16,16,4096]{2,1,0:T(8,128)(2,1)} %scatter_fusion), calls=%async_computation | async-start | bytes 4194304 | tf_op jit(solution)/shard_map/all_to_all | solution.py:120
  348.8 7.1 %copy-start.3 = (bf16[12,3,4096]{2,1,0:T(4,128)(2,1)}, bf16[12,3,4096]{2,1,0:T(4,128)(2,1)S(1)}, u32[]{:S(2)}) copy-start(bf16[12,3,4096]{2,1,0:T(4,128)(2,1)S(1)} %scatter_fusion.3) | copy-start | bytes 884740
Sparse Core Ops, SparseCore 0:
  16.1 22.7 all-reduce.1
where the time goes:
time: 367 us; the launch traced here: 363 us
  other arithmetic  146 us (40%)
  local copies, waits for them, and re-layouts  68.9 us (19%)
  blocking collectives  65.5 us (18%)
  loops' own time  41.6 us (11%)
  between operations  15.7 us (4%)
  starting transfers between devices  12.3 us (3%)
  waiting for transfers between devices  6.96 us (2%)
  matrix products  5.99 us (2%)
    psum x1, blocking collectives, per_device(): totals = lax.psum(partial_sums, 'req')  65.5 us
    reduce_sum x16, other arithmetic, advance(): jnp.sum(out_float[:, position, :, None] * hidden, axis=1) + skip * conv_now  56.6 us
    another operation x1, loops' own time, per_device(): lax.scan(advance, (initial, kept_first), jnp.arange(drafts, dtype=jnp.int...  41.6 us
    select_n x16, other arithmetic, advance(): jnp.where((accepted == position + 1)[:, None, None], hidden, kept_state)  31 us
    dynamic_update_slice x16, other arithmetic, per_device(): lax.scan(advance, (initial, kept_first), jnp.arange(drafts, dtype=jnp.int...  25.2 us
    dynamic_slice x16, local copies, waits for them, and re-layouts, advance(): size_now = step_size[:, position, :]  21.2 us
    mul x16, other arithmetic, advance(): decay_now = jnp.exp(size_now[:, None, :] * decay_rate[None, :, :])  16 us
    mul x16, local copies, waits for them, and re-layouts, advance(): out_float[:, position, :, None] * hidden  11.1 us
  transfers between devices with their start and end apart: 3, of which 1 were waited for; matrix products, arithmetic and copies ran while one was open for 56% of the time, Pallas kernels for 0%

commit v1 on v0

--- a/solution.py
+++ b/solution.py
@@ -138,7 +138,9 @@
     accept_sum = jnp.sum(jnp.where(inside, accepted_float[None, :], 0.0), axis=1)
     length_sum = jnp.sum(jnp.where(inside, new_length[None, :], 0.0), axis=1)
     partial_sums = jnp.stack([accept_sum, length_sum], axis=1)
-    totals = lax.psum(partial_sums, "req")
+    totals = partial_sums
+    for hop in (1, 2, 4, 8):
+        totals = totals + lax.ppermute(totals, "req", [(dev, dev ^ hop) for dev in range(16)])
     members = (tenant_range[:, 1] - tenant_range[:, 0]).astype(jnp.float32)
     accept_rate = totals[:, 0] / (STEPS * members)
     length_load = totals[:, 1] / members / (jnp.sum(totals[:, 1]) / jnp.sum(members))

time: 367 us -> 349 us (0.951)
  the two profiles are of different devices: /device:TPU:16 before, /device:TPU:0 now
where the time goes in v1:
time: 349 us; the launch traced here: 345 us
  other arithmetic  146 us (42%)
  local copies, waits for them, and re-layouts  68.7 us (20%)
  waiting for transfers between devices  46.4 us (13%)
  loops' own time  41.6 us (12%)
  starting transfers between devices  20.3 us (6%)
  between operations  15.7 us (4%)
  matrix products  5.99 us (2%)
    reduce_sum x16, other arithmetic, advance(): jnp.sum(out_float[:, position, :, None] * hidden, axis=1) + skip * conv_now  56.6 us
    another operation x1, loops' own time, per_device(): lax.scan(advance, (initial, kept_first), jnp.arange(drafts, dtype=jnp.int...  41.6 us
    ppermute x4, waiting for transfers between devices, per_device(): lax.ppermute(totals, 'req', [(dev, dev ^ hop) for dev in range(16)])  39.1 us
    select_n x16, other arithmetic, advance(): jnp.where((accepted == position + 1)[:, None, None], hidden, kept_state)  31 us
    dynamic_update_slice x16, other arithmetic, per_device(): lax.scan(advance, (initial, kept_first), jnp.arange(drafts, dtype=jnp.int...  25.2 us
    dynamic_slice x16, local copies, waits for them, and re-layouts, advance(): size_now = step_size[:, position, :]  21.2 us
    mul x16, other arithmetic, advance(): decay_now = jnp.exp(size_now[:, None, :] * decay_rate[None, :, :])  16 us
    mul x16, local copies, waits for them, and re-layouts, advance(): out_float[:, position, :, None] * hidden  11.1 us
  transfers between devices with their start and end apart: 7, of which 4 were waited for; matrix products, arithmetic and copies ran while one was open for 59% of the time, Pallas kernels for 0%

profile of v1, /device:TPU:0, one launch (start us, length us, event | category | flops | bytes accessed | tf_op | source)
XLA Modules:
  0.0 344.5 jit_solution(13394112378421166936)
XLA Ops:
  22.1 7.4 %all-to-all-start.1 = ((bf16[16,3,4096]{2,1,0:T(4,128)(2,1)}), bf16[16,3,4096]{2,1,0:T(4,128)(2,1)}, u32[]{:S(2)}, u32[]{:S(2)}) async-start(bf16[16,3,4096]{2,1,0:T(4,128)(2,1)} %scatter_fusion.2), calls=%async_computation.1 | async-start | bytes 1048576 | tf_op jit(solution)/shard_map/all_to_all | solution.py:121
  33.2 7.3 %all-reduce.2.cloned.1.call-done = f32[128,288]{0,1:T(8,128)} async-done(((f32[128,288]{0,1:T(8,128)}), f32[128,288]{0,1:T(8,128)}) %all-reduce.2.cloned.1.call-update) | async-done | bytes 147472 | tf_op jit(solution)/shard_map/psum | solution.py:90
  44.0 4.5 %compare_select_fusion = f32[128,4096]{1,0:T(8,128)} fusion(bf16[256,4096]{1,0:T(8,128)(2,1)} %param.29, f32[4096]{0:T(1024)} %param.30, f32[128,288]{0,1:T(8,128)} %all-reduce.2.cloned.1.call-done, f32[256]{0:T(256)} %param.26, f32[128]{0:T(128)S(1)} %add_rsqrt_fusion), kind=kOutput, calls=%fused_computation.17 | convolution fusion | flops 272203776 | bytes 4343296 | tf_op jit(solution)/shard_map/dot_general | solution.py:93
  48.6 212.8 %while.14 = (s32[]{:T(128)}, f32[8,16,4096]{2,1,0:T(8,128)}, bf16[8,16,4096]{2,1,0:T(8,128)(2,1)S(1)}, f32[16,8,4096]{2,1,0:T(8,128)}, s32[16]{0:T(128)S(1)}, /*...) while((s32[]{:T(128)}, f32[8,16,4096]{2,1,0:T(8,128)}, ...), condition=%wide.region_6.7_spmd, body=%wide.region_4.6_spmd.sunk | while | flops 3735566 | bytes 10243851 | solution.py:115
  54.2 3.5 %multiply_reduce_fusion.5 = (f32[8,4096]{1,0:T(8,128)S(1)}, f32[8,16,4096]{2,1,0:T(8,128)}) fusion(f32[8,16]{1,0:T(8,128)S(1)} %get-tuple-element.238, f32[8,16]{1,0:T(8,128)S(1)} %get-tuple-element.239, f32[8,4096]{1,0:T(8,128)S(1)} %get-tuple-element.240, f32[8,16,4096]{2,1,0:T(8,128)} %get-tuple-element.260, f32[16,4096]{1,0:T(8,128)} %get-tuple-element.280, ...), kind=kLoop, calls=%fused_computation.5.clone.1 | loop fusion | flops 3112960 | bytes 4850688 | tf_op jit(solution)/shard_map/while/body/eval_jaxpr/reduce_sum | solution.py:111
  67.5 3.5 %multiply_reduce_fusion.5 = (f32[8,4096]{1,0:T(8,128)S(1)}, f32[8,16,4096]{2,1,0:T(8,128)}) fusion(f32[8,16]{1,0:T(8,128)S(1)} %get-tuple-element.238, f32[8,16]{1,0:T(8,128)S(1)} %get-tuple-element.239, f32[8,4096]{1,0:T(8,128)S(1)} %get-tuple-element.240, f32[8,16,4096]{2,1,0:T(8,128)} %get-tuple-element.260, f32[16,4096]{1,0:T(8,128)} %get-tuple-element.280, ...), kind=kLoop, calls=%fused_computation.5.clone.1 | loop fusion | flops 3112960 | bytes 4850688 | tf_op jit(solution)/shard_map/while/body/eval_jaxpr/reduce_sum | solution.py:111
  80.8 3.5 %multiply_reduce_fusion.5 = (f32[8,4096]{1,0:T(8,128)S(1)}, f32[8,16,4096]{2,1,0:T(8,128)}) fusion(f32[8,16]{1,0:T(8,128)S(1)} %get-tuple-element.238, f32[8,16]{1,0:T(8,128)S(1)} %get-tuple-element.239, f32[8,4096]{1,0:T(8,128)S(1)} %get-tuple-element.240, f32[8,16,4096]{2,1,0:T(8,128)} %get-tuple-element.260, f32[16,4096]{1,0:T(8,128)} %get-tuple-element.280, ...), kind=kLoop, calls=%fused_computation.5.clone.1 | loop fusion | flops 3112960 | bytes 4850688 | tf_op jit(solution)/shard_map/while/body/eval_jaxpr/reduce_sum | solution.py:111
  94.1 3.5 %multiply_reduce_fusion.5 = (f32[8,4096]{1,0:T(8,128)S(1)}, f32[8,16,4096]{2,1,0:T(8,128)}) fusion(f32[8,16]{1,0:T(8,128)S(1)} %get-tuple-element.238, f32[8,16]{1,0:T(8,128)S(1)} %get-tuple-element.239, f32[8,4096]{1,0:T(8,128)S(1)} %get-tuple-element.240, f32[8,16,4096]{2,1,0:T(8,128)} %get-tuple-element.260, f32[16,4096]{1,0:T(8,128)} %get-tuple-element.280, ...), kind=kLoop, calls=%fused_computation.5.clone.1 | loop fusion | flops 3112960 | bytes 4850688 | tf_op jit(solution)/shard_map/while/body/eval_jaxpr/reduce_sum | solution.py:111
  107.4 3.5 %multiply_reduce_fusion.5 = (f32[8,4096]{1,0:T(8,128)S(1)}, f32[8,16,4096]{2,1,0:T(8,128)}) fusion(f32[8,16]{1,0:T(8,128)S(1)} %get-tuple-element.238, f32[8,16]{1,0:T(8,128)S(1)} %get-tuple-element.239, f32[8,4096]{1,0:T(8,128)S(1)} %get-tuple-element.240, f32[8,16,4096]{2,1,0:T(8,128)} %get-tuple-element.260, f32[16,4096]{1,0:T(8,128)} %get-tuple-element.280, ...), kind=kLoop, calls=%fused_computation.5.clone.1 | loop fusion | flops 3112960 | bytes 4850688 | tf_op jit(solution)/shard_map/while/body/eval_jaxpr/reduce_sum | solution.py:111
  120.7 3.5 %multiply_reduce_fusion.5 = (f32[8,4096]{1,0:T(8,128)S(1)}, f32[8,16,4096]{2,1,0:T(8,128)}) fusion(f32[8,16]{1,0:T(8,128)S(1)} %get-tuple-element.238, f32[8,16]{1,0:T(8,128)S(1)} %get-tuple-element.239, f32[8,4096]{1,0:T(8,128)S(1)} %get-tuple-element.240, f32[8,16,4096]{2,1,0:T(8,128)} %get-tuple-element.260, f32[16,4096]{1,0:T(8,128)} %get-tuple-element.280, ...), kind=kLoop, calls=%fused_computation.5.clone.1 | loop fusion | flops 3112960 | bytes 4850688 | tf_op jit(solution)/shard_map/while/body/eval_jaxpr/reduce_sum | solution.py:111
  134.0 3.5 %multiply_reduce_fusion.5 = (f32[8,4096]{1,0:T(8,128)S(1)}, f32[8,16,4096]{2,1,0:T(8,128)}) fusion(f32[8,16]{1,0:T(8,128)S(1)} %get-tuple-element.238, f32[8,16]{1,0:T(8,128)S(1)} %get-tuple-element.239, f32[8,4096]{1,0:T(8,128)S(1)} %get-tuple-element.240, f32[8,16,4096]{2,1,0:T(8,128)} %get-tuple-element.260, f32[16,4096]{1,0:T(8,128)} %get-tuple-element.280, ...), kind=kLoop, calls=%fused_computation.5.clone.1 | loop fusion | flops 3112960 | bytes 4850688 | tf_op jit(solution)/shard_map/while/body/eval_jaxpr/reduce_sum | solution.py:111
  147.3 3.5 %multiply_reduce_fusion.5 = (f32[8,4096]{1,0:T(8,128)S(1)}, f32[8,16,4096]{2,1,0:T(8,128)}) fusion(f32[8,16]{1,0:T(8,128)S(1)} %get-tuple-element.238, f32[8,16]{1,0:T(8,128)S(1)} %get-tuple-element.239, f32[8,4096]{1,0:T(8,128)S(1)} %get-tuple-element.240, f32[8,16,4096]{2,1,0:T(8,128)} %get-tuple-element.260, f32[16,4096]{1,0:T(8,128)} %get-tuple-element.280, ...), kind=kLoop, calls=%fused_computation.5.clone.1 | loop fusion | flops 3112960 | bytes 4850688 | tf_op jit(solution)/shard_map/while/body/eval_jaxpr/reduce_sum | solution.py:111
  160.6 3.5 %multiply_reduce_fusion.5 = (f32[8,4096]{1,0:T(8,128)S(1)}, f32[8,16,4096]{2,1,0:T(8,128)}) fusion(f32[8,16]{1,0:T(8,128)S(1)} %get-tuple-element.238, f32[8,16]{1,0:T(8,128)S(1)} %get-tuple-element.239, f32[8,4096]{1,0:T(8,128)S(1)} %get-tuple-element.240, f32[8,16,4096]{2,1,0:T(8,128)} %get-tuple-element.260, f32[16,4096]{1,0:T(8,128)} %get-tuple-element.280, ...), kind=kLoop, calls=%fused_computation.5.clone.1 | loop fusion | flops 3112960 | bytes 4850688 | tf_op jit(solution)/shard_map/while/body/eval_jaxpr/reduce_sum | solution.py:111
  173.9 3.5 %multiply_reduce_fusion.5 = (f32[8,4096]{1,0:T(8,128)S(1)}, f32[8,16,4096]{2,1,0:T(8,128)}) fusion(f32[8,16]{1,0:T(8,128)S(1)} %get-tuple-element.238, f32[8,16]{1,0:T(8,128)S(1)} %get-tuple-element.239, f32[8,4096]{1,0:T(8,128)S(1)} %get-tuple-element.240, f32[8,16,4096]{2,1,0:T(8,128)} %get-tuple-element.260, f32[16,4096]{1,0:T(8,128)} %get-tuple-element.280, ...), kind=kLoop, calls=%fused_computation.5.clone.1 | loop fusion | flops 3112960 | bytes 4850688 | tf_op jit(solution)/shard_map/while/body/eval_jaxpr/reduce_sum | solution.py:111
  187.2 3.5 %multiply_reduce_fusion.5 = (f32[8,4096]{1,0:T(8,128)S(1)}, f32[8,16,4096]{2,1,0:T(8,128)}) fusion(f32[8,16]{1,0:T(8,128)S(1)} %get-tuple-element.238, f32[8,16]{1,0:T(8,128)S(1)} %get-tuple-element.239, f32[8,4096]{1,0:T(8,128)S(1)} %get-tuple-element.240, f32[8,16,4096]{2,1,0:T(8,128)} %get-tuple-element.260, f32[16,4096]{1,0:T(8,128)} %get-tuple-element.280, ...), kind=kLoop, calls=%fused_computation.5.clone.1 | loop fusion | flops 3112960 | bytes 4850688 | tf_op jit(solution)/shard_map/while/body/eval_jaxpr/reduce_sum | solution.py:111
  200.5 3.5 %multiply_reduce_fusion.5 = (f32[8,4096]{1,0:T(8,128)S(1)}, f32[8,16,4096]{2,1,0:T(8,128)}) fusion(f32[8,16]{1,0:T(8,128)S(1)} %get-tuple-element.238, f32[8,16]{1,0:T(8,128)S(1)} %get-tuple-element.239, f32[8,4096]{1,0:T(8,128)S(1)} %get-tuple-element.240, f32[8,16,4096]{2,1,0:T(8,128)} %get-tuple-element.260, f32[16,4096]{1,0:T(8,128)} %get-tuple-element.280, ...), kind=kLoop, calls=%fused_computation.5.clone.1 | loop fusion | flops 3112960 | bytes 4850688 | tf_op jit(solution)/shard_map/while/body/eval_jaxpr/reduce_sum | solution.py:111
  213.8 3.5 %multiply_reduce_fusion.5 = (f32[8,4096]{1,0:T(8,128)S(1)}, f32[8,16,4096]{2,1,0:T(8,128)}) fusion(f32[8,16]{1,0:T(8,128)S(1)} %get-tuple-element.238, f32[8,16]{1,0:T(8,128)S(1)} %get-tuple-element.239, f32[8,4096]{1,0:T(8,128)S(1)} %get-tuple-element.240, f32[8,16,4096]{2,1,0:T(8,128)} %get-tuple-element.260, f32[16,4096]{1,0:T(8,128)} %get-tuple-element.280, ...), kind=kLoop, calls=%fused_computation.5.clone.1 | loop fusion | flops 3112960 | bytes 4850688 | tf_op jit(solution)/shard_map/while/body/eval_jaxpr/reduce_sum | solution.py:111
  265.8 5.9 %all-to-all-start = ((bf16[16,16,4096]{2,1,0:T(8,128)(2,1)}), bf16[16,16,4096]{2,1,0:T(8,128)(2,1)}, u32[]{:S(2)}, u32[]{:S(2)}) async-start(bf16[16,16,4096]{2,1,0:T(8,128)(2,1)} %scatter_fusion), calls=%async_computation | async-start | bytes 4194304 | tf_op jit(solution)/shard_map/all_to_all | solution.py:120
  276.8 7.4 %collective-permute-done.1 = f32[4,2]{0,1:T(2,128)S(1)} collective-permute-done((f32[4,2]{0,1:T(2,128)S(1)}, f32[4,2]{0,1:T(2,128)S(1)}, u32[]{:S(2)}, u32[]{:S(2)}) %collective-permute-start.1) | collective-permute-done | bytes 64 | tf_op jit(solution)/shard_map/ppermute | solution.py:143
  284.8 21.9 %collective-permute-done.2 = f32[4,2]{0,1:T(2,128)S(1)} collective-permute-done((f32[4,2]{0,1:T(2,128)S(1)}, f32[4,2]{0,1:T(2,128)S(1)}, u32[]{:S(2)}, u32[]{:S(2)}) %collective-permute-start.2) | collective-permute-done | bytes 64 | tf_op jit(solution)/shard_map/ppermute | solution.py:143
  306.7 4.3 %collective-permute-start.3 = (f32[4,2]{0,1:T(2,128)S(1)}, f32[4,2]{0,1:T(2,128)S(1)}, u32[]{:S(2)}, u32[]{:S(2)}) collective-permute-start(f32[4,2]{0,1:T(2,128)S(1)} %add.205), channel_id=1, source_target_pairs={{0,16},{2,18},{4,20},{6,22},{8,24},{10,26},{12,28},{14,30},{16,0},... | collective-permute-start | bytes 104 | tf_op jit(solution)/shard_map/ppermute | solution.py:143
  311.0 9.7 %collective-permute-done.3 = f32[4,2]{0,1:T(2,128)S(1)} collective-permute-done((f32[4,2]{0,1:T(2,128)S(1)}, f32[4,2]{0,1:T(2,128)S(1)}, u32[]{:S(2)}, u32[]{:S(2)}) %collective-permute-start.3) | collective-permute-done | bytes 64 | tf_op jit(solution)/shard_map/ppermute | solution.py:143
  323.3 3.6 %fusion.2 = bf16[8,16,4096]{2,0,1:T(8,128)(2,1)S(1)} fusion(f32[16,8,4096]{2,1,0:T(8,128)} %get-tuple-element.67, f32[8,16,4096]{2,1,0:T(8,128)} %convert.4), kind=kLoop, calls=%fused_computation.20 | loop fusion | flops 3145728 | bytes 5242880 | tf_op jit(solution)/shard_map/convert_element_type | solution.py:127
  332.0 5.7 %scatter_fusion.1 = bf16[12,16,4096]{2,1,0:T(8,128)(2,1)} fusion(bf16[12,16,4096]{2,1,0:T(8,128)(2,1)} %broadcast_in_dim.97, s32[16]{0:T(128)S(1)} %fusion.5, bf16[16,16,4096]{2,1,0:T(8,128)(2,1)} %all-to-all-done), kind=kCustom, calls=%fused_computation.2 | custom fusion | bytes 6291520 | tf_op jit(solution)/shard_map/scatter | solution.py:80
  (212 shorter events, 163.4 us)
Async XLA Ops:
  7.2 7.3 %copy-start = (bf16[4096,288]{0,1:T(8,128)(2,1)S(1)}, bf16[4096,288]{0,1:T(8,128)(2,1)}, u32[]{:S(2)}) copy-start(bf16[4096,288]{0,1:T(8,128)(2,1)} %param.25) | copy-start | bytes 7077892
  7.2 4.0 %copy-start.2 = (bf16[128,4096]{1,0:T(8,128)(2,1)S(1)}, bf16[128,4096]{1,0:T(8,128)(2,1)}, u32[]{:S(2)}) copy-start(bf16[128,4096]{1,0:T(8,128)(2,1)} %param.20) | copy-start | bytes 3145732
  7.2 4.0 %copy-start.7 = (f32[4096]{0:T(1024)S(1)}, f32[4096]{0:T(1024)}, u32[]{:S(2)}) copy-start(f32[4096]{0:T(1024)} %param.24) | copy-start | bytes 49156
  7.2 33.3 %all-reduce.2.cloned.1.call-start = ((), (), s32[]{:S(2)}) async-start(), calls=%async_computation.2 | async-start | bytes 294912 | tf_op jit(solution)/shard_map/psum | solution.py:90
  11.2 2.7 copy-start.1
  14.4 1.5 copy-start.9
  14.5 1.7 copy-start.13
  22.1 243.7 %all-to-all-start.1 = ((bf16[16,3,4096]{2,1,0:T(4,128)(2,1)}), bf16[16,3,4096]{2,1,0:T(4,128)(2,1)}, u32[]{:S(2)}, u32[]{:S(2)}) async-start(bf16[16,3,4096]{2,1,0:T(4,128)(2,1)} %scatter_fusion.2), calls=%async_computation.1 | async-start | bytes 1048576 | tf_op jit(solution)/shard_map/all_to_all | solution.py:121
  29.5 2.9 copy-start.6
  29.6 11.7 %copy-start.10 = (f32[16]{0:T(128)S(1)}, f32[16]{0:T(128)}, u32[]{:S(2)}) copy-start(f32[16]{0:T(128)} %param.28) | copy-start | bytes 196
  29.6 11.7 %copy-start.11 = (f32[16]{0:T(128)S(1)}, f32[16]{0:T(128)}, u32[]{:S(2)}) copy-start(f32[16]{0:T(128)} %param.27) | copy-start | bytes 196
  44.0 4.6 %copy-start.5 = (f32[4096]{0:T(1024)S(1)}, f32[4096]{0:T(1024)}, u32[]{:S(2)}) copy-start(f32[4096]{0:T(1024)} %param.32) | copy-start | bytes 49156
  265.8 5.9 %copy-start.8 = (s32[4,2]{0,1:T(2,128)S(1)}, s32[4,2]{0,1:T(2,128)}, u32[]{:S(2)}) copy-start(s32[4,2]{0,1:T(2,128)} %param.36) | copy-start | bytes 100
  265.8 5.9 %copy-start.12 = (s32[8]{0:T(128)S(1)}, s32[8]{0:T(128)}, u32[]{:S(2)}) copy-start(s32[8]{0:T(128)} %param.35) | copy-start | bytes 100
  265.8 6.6 %copy-start.14 = (s32[128]{0:T(128)S(1)}, s32[128]{0:T(128)}, u32[]{:S(2)}) copy-start(s32[128]{0:T(128)} %param.37) | copy-start | bytes 1540
  265.8 7.0 %copy-start.4 = (bf16[128,4096]{1,0:T(8,128)(2,1)S(1)}, bf16[128,4096]{1,0:T(8,128)(2,1)}, u32[]{:S(2)}) copy-start(bf16[128,4096]{1,0:T(8,128)(2,1)} %param.21) | copy-start | bytes 3145732
  265.8 64.8 %all-to-all-start = ((bf16[16,16,4096]{2,1,0:T(8,128)(2,1)}), bf16[16,16,4096]{2,1,0:T(8,128)(2,1)}, u32[]{:S(2)}, u32[]{:S(2)}) async-start(bf16[16,16,4096]{2,1,0:T(8,128)(2,1)} %scatter_fusion), calls=%async_computation | async-start | bytes 4194304 | tf_op jit(solution)/shard_map/all_to_all | solution.py:120
  272.0 3.1 collective-permute-start
  275.1 9.2 %collective-permute-start.1 = (f32[4,2]{0,1:T(2,128)S(1)}, f32[4,2]{0,1:T(2,128)S(1)}, u32[]{:S(2)}, u32[]{:S(2)}) collective-permute-start(f32[4,2]{0,1:T(2,128)S(1)} %fusion.15), channel_id=1, source_target_pairs={{0,4},{2,6},{4,0},{6,2},{8,12},{10,14},{12,8},{14,10},{16,20},{18,... | collective-permute-start | bytes 104 | tf_op jit(solution)/shard_map/ppermute | solution.py:143
  284.3 22.4 %collective-permute-start.2 = (f32[4,2]{0,1:T(2,128)S(1)}, f32[4,2]{0,1:T(2,128)S(1)}, u32[]{:S(2)}, u32[]{:S(2)}) collective-permute-start(f32[4,2]{0,1:T(2,128)S(1)} %fusion.23), channel_id=1, source_target_pairs={{0,8},{2,10},{4,12},{6,14},{8,0},{10,2},{12,4},{14,6},{16,24},{18,... | collective-permute-start | bytes 104 | tf_op jit(solution)/shard_map/ppermute | solution.py:143
  306.7 14.1 %collective-permute-start.3 = (f32[4,2]{0,1:T(2,128)S(1)}, f32[4,2]{0,1:T(2,128)S(1)}, u32[]{:S(2)}, u32[]{:S(2)}) collective-permute-start(f32[4,2]{0,1:T(2,128)S(1)} %add.205), channel_id=1, source_target_pairs={{0,16},{2,18},{4,20},{6,22},{8,24},{10,26},{12,28},{14,30},{16,0},... | collective-permute-start | bytes 104 | tf_op jit(solution)/shard_map/ppermute | solution.py:143
  330.6 7.0 %copy-start.3 = (bf16[12,3,4096]{2,1,0:T(4,128)(2,1)}, bf16[12,3,4096]{2,1,0:T(4,128)(2,1)S(1)}, u32[]{:S(2)}) copy-start(bf16[12,3,4096]{2,1,0:T(4,128)(2,1)S(1)} %scatter_fusion.3) | copy-start | bytes 884740
Sparse Core Ops, SparseCore 0:
  16.1 24.4 all-reduce.1
